TPU v7x, 32 devices: a whole 2x2x4 slice. The times are simulated.
32 devices in a mesh: wide: 8 (over y, x, core), narrow: 4 (over z).
Axes of the slice: x: 2, y: 2, z: 4, core: 2. Of those that a mesh axis runs over, the one named last changes fastest.
Arguments:
- hidden: bfloat16 [8, 256, 2048], P('wide', None, 'narrow'), may hold values from -6 to 6
- norm_gain: bfloat16 [2, 2048], replicated, may hold values from 0.25 to 1.75
- w_qkv: bfloat16 [2048, 3, 2048], P(None, None, 'narrow'), may hold values from -1 to 1
- qk_gain: float32 [2, 2048], P(None, 'narrow'), may hold values from 0.25 to 32
- w_out: bfloat16 [2048, 2048], P('narrow'), may hold values from -0.125 to 0.125
- cache: bfloat16 [2, 8, 2048, 2048], P(None, 'wide', None, 'narrow'), may hold values from -6 to 6
- lengths: int32 [8], replicated, may hold values from 1 to 2048, 8192 in all
- placing: int32 [8], replicated, may hold values from 0 to 7, each once
- routes: int32 [8, 256, 8], P('wide'), may hold values from 0 to 15, all different within a row; in each aligned block of 256 rows (0 to 255, 256 to 511, ..., all dimensions but the last counted through in order) at most 192 rows name the same one
- gate_w: float32 [8, 256, 8], P('wide'), may hold values from 0.02 to 0.3
- w_gu: bfloat16 [16, 2048, 2, 1024], P('wide', None, None, 'narrow'), may hold values from -0.125 to 0.125
- w_down: bfloat16 [16, 1024, 2048], P('wide', 'narrow'), may hold values from -0.1875 to 0.1875
Outputs:
- result: bfloat16 [8, 256, 2048], P('wide', None, 'narrow')
- new_cache: bfloat16 [2, 8, 256, 2048], P(None, 'wide', None, 'narrow')
Inputs may be any that keep to these rules, and one draw needn't show every extreme that they name: `routes`: each token names 8 different experts; among the 256 tokens of one request no expert is named more than 192 times. `lengths`: some request has 2048 cached positions. Slot s holds request placing[s]; every request is held once.
All inputs are finite; a program needn't handle non-finite values.
Results may differ from a plain program's by a relative error of at most 0.013.
Values may be sent and summed in bfloat16 or wider, within the bound.
A program may use at most 128 MiB of HBM per device.

v0:
```python
import jax
import jax.numpy as jnp
from jax import lax
from jax.sharding import PartitionSpec as P

HD = 128


def normalize(values, gain_row):
    values = values.astype(jnp.float32)
    return (
        values
        * lax.rsqrt(jnp.mean(values * values, axis=-1, keepdims=True) + 1e-05)
        * gain_row.astype(jnp.float32)
    )


def rotary(values, positions):
    half_dim = values.shape[-1] // 2
    frequency = 10000.0 ** (-(jnp.arange(half_dim, dtype=jnp.float32) * (2.0 / values.shape[-1])))
    angle = positions[:, None] * frequency[None, :]
    cosine = jnp.cos(angle)[:, None, :]
    sine_part = jnp.sin(angle)[:, None, :]
    first_half = values[..., :half_dim]
    second_half = values[..., half_dim:]
    return jnp.concatenate(
        [
            first_half * cosine - second_half * sine_part,
            second_half * cosine + first_half * sine_part,
        ],
        axis=-1,
    )


def per_device(
    hidden, norm_gain, w_qkv, qk_gain, w_out, cache, lengths, placing, routes, gate_w, w_gu, w_down
):
    narrow = lax.axis_size("narrow")
    wide_size = lax.axis_size("wide")
    column = lax.axis_index("narrow")
    position = lax.axis_index("wide")
    span_len = hidden.shape[1]
    share_cols = hidden.shape[2]
    full_width = share_cols * narrow
    tokens = lax.all_gather(hidden[0], "narrow", axis=1, tiled=True)
    normed = normalize(tokens, norm_gain[0]).astype(jnp.bfloat16)
    local_cols = w_qkv.shape[2]
    projected = jnp.dot(
        normed, w_qkv.reshape(full_width, 3 * local_cols), preferred_element_type=jnp.float32
    )
    queries = projected[:, :local_cols]
    keys_new = projected[:, local_cols : 2 * local_cols]
    values_new = projected[:, 2 * local_cols :]
    squares = lax.psum((jnp.sum(queries * queries, -1), jnp.sum(keys_new * keys_new, -1)), "narrow")
    features = local_cols * narrow
    queries = queries * lax.rsqrt(squares[0][:, None] / features + 1e-05) * qk_gain[0]
    keys_new = keys_new * lax.rsqrt(squares[1][:, None] / features + 1e-05) * qk_gain[1]
    head_count = local_cols // HD
    length = lengths[placing[position]]
    positions = length.astype(jnp.float32) + jnp.arange(span_len, dtype=jnp.float32)
    queries = rotary(queries.reshape(span_len, head_count, HD), positions).astype(jnp.bfloat16)
    keys_new = rotary(keys_new.reshape(span_len, head_count, HD), positions).astype(jnp.bfloat16)
    values_new = values_new.reshape(span_len, head_count, HD).astype(jnp.bfloat16)
    stored = cache.shape[2]
    all_keys = jnp.concatenate([cache[0, 0].reshape(stored, head_count, HD), keys_new], 0)
    all_values = jnp.concatenate([cache[1, 0].reshape(stored, head_count, HD), values_new], 0)
    scores = jnp.einsum(
        "thd,jhd->htj", queries, all_keys, preferred_element_type=jnp.float32
    ) * HD ** (-0.5)
    key_index = jnp.arange(stored + span_len, dtype=jnp.int32)[None, :]
    query_index = jnp.arange(span_len, dtype=jnp.int32)[:, None]
    allowed = jnp.where(key_index < stored, key_index < length, key_index - stored <= query_index)
    scores = jnp.where(allowed[None], scores, -1e30)
    highest = jnp.max(scores, axis=-1, keepdims=True)
    exponent = jnp.exp(scores - highest)
    weights = exponent.astype(jnp.bfloat16)
    denominator = jnp.sum(exponent, axis=-1)
    summed = jnp.einsum("htj,jhd->thd", weights, all_values, preferred_element_type=jnp.float32)
    heads_out = (
        (summed / jnp.transpose(denominator)[:, :, None])
        .astype(jnp.bfloat16)
        .reshape(span_len, local_cols)
    )
    partial_out = jnp.dot(heads_out, w_out, preferred_element_type=jnp.float32)
    attention = lax.psum(partial_out.astype(jnp.bfloat16), "narrow").astype(jnp.float32)
    after = (tokens.astype(jnp.float32) + attention).astype(jnp.bfloat16)
    after_own = lax.dynamic_slice_in_dim(after, column * share_cols, share_cols, 1)
    routed = normalize(after, norm_gain[1]).astype(jnp.bfloat16)
    chosen = routes.shape[2]
    held_experts = w_gu.shape[0]
    experts = held_experts * wide_size
    capacity = span_len * chosen * 3 // (2 * experts)
    flat_routes = routes[0].reshape(-1)
    onehot = (flat_routes[:, None] == jnp.arange(experts, dtype=jnp.int32)[None, :]).astype(
        jnp.int32
    )
    slot_rank = jnp.sum((jnp.cumsum(onehot, 0) - onehot) * onehot, 1)
    target = flat_routes * capacity + slot_rank
    token_row = jnp.arange(span_len * chosen, dtype=jnp.int32) // chosen
    source_row = jnp.full((experts * capacity,), span_len, jnp.int32).at[target].set(token_row)
    padded = jnp.concatenate([routed, jnp.zeros((1, full_width), jnp.bfloat16)], 0)
    outgoing = padded[source_row].reshape(experts, capacity, full_width)
    arrived = lax.all_to_all(outgoing, "wide", split_axis=0, concat_axis=0, tiled=True)
    inner_cols = w_gu.shape[3]
    arrived = arrived.reshape(wide_size, held_experts, capacity, full_width)
    gate_up = jnp.einsum(
        "wjcd,jdf->wjcf",
        arrived,
        w_gu.reshape(held_experts, full_width, 2 * inner_cols),
        preferred_element_type=jnp.float32,
    )
    activated = (jax.nn.silu(gate_up[..., :inner_cols]) * gate_up[..., inner_cols:]).astype(
        jnp.bfloat16
    )
    parts = jnp.einsum(
        "wjcf,jfd->wjcd", activated, w_down, preferred_element_type=jnp.float32
    ).astype(jnp.bfloat16)
    gate_scale = gate_w[0].reshape(-1)
    returned = lax.all_to_all(
        parts.reshape(experts, capacity, full_width),
        "wide",
        split_axis=0,
        concat_axis=0,
        tiled=True,
    )
    picked = returned.reshape(experts * capacity, full_width)[target].astype(jnp.float32)
    combined = jnp.sum((picked * gate_scale[:, None]).reshape(span_len, chosen, full_width), 1)
    expert_out = lax.psum_scatter(
        combined.astype(jnp.bfloat16), "narrow", scatter_dimension=1, tiled=True
    ).astype(jnp.float32)
    result = (after_own.astype(jnp.float32) + expert_out).astype(jnp.bfloat16)[None]
    fresh = jnp.stack(
        [keys_new.reshape(span_len, local_cols), values_new.reshape(span_len, local_cols)]
    )[:, None]
    return (result, fresh)


def solution(mesh):
    placed = (
        P("wide", None, "narrow"),
        P(),
        P(None, None, "narrow"),
        P(None, "narrow"),
        P("narrow", None),
        P(None, "wide", None, "narrow"),
        P(),
        P(),
        P("wide", None, None),
        P("wide", None, None),
        P("wide", None, None, "narrow"),
        P("wide", "narrow", None),
    )
    return jax.shard_map(
        per_device,
        mesh=mesh,
        in_specs=placed,
        out_specs=(P("wide", None, "narrow"), P(None, "wide", None, "narrow")),
        check_vma=False,
    )
```

profile of v0, /device:TPU:0, one launch (start us, length us, event | category | flops | bytes accessed | tf_op | source)
XLA Modules:
  0.0 548.3 jit_solution(7301213833029315441)
XLA Ops:
  7.2 0.7 all-gather.3.cloned.1.call-update
  8.0 1.2 dynamic_slice.9
  11.2 1.2 dynamic_slice.10
  13.1 0.7 iota_compare_fusion.3
  13.7 0.8 copy.33
  14.6 0.7 broadcast_multiply_fusion
  15.3 8.9 %copy.24 = bf16[2048,3,512]{0,2,1:T(8,128)(2,1)} copy(bf16[2048,3,512]{2,0,1:T(8,128)(2,1)} %param.14) | data formatting | bytes 12582912 | tf_op args[2]
  24.2 4.5 fusion.74
  28.7 4.0 copy.45
  32.7 4.0 copy.31
  36.7 4.0 copy.23
  40.8 4.5 reduce-window.6
  46.8 1.5 fusion.27
  48.3 5.0 fusion.39
  53.4 1.0 copy-done.2
  54.5 0.7 slice.97
  55.2 13.6 %all-reduce.1 = (f32[256]{0:T(256)S(1)}, f32[256]{0:T(256)S(1)}) all-reduce(f32[256]{0:T(256)S(1)} %get-tuple-element.7, f32[256]{0:T(256)S(1)} %get-tuple-element.6), channel_id=1, replica_groups=mesh['wide'=8,'narrow'=4] {'narrow'}, use_global_device_ids=true, to_apply=%region_4.0 | all-reduce | flops 512 | bytes 4096 | tf_op jit(solution)/shard_map/psum | solution.py:54
  68.9 2.3 multiply_multiply_fusion.1
  71.2 1.2 reshape.249
  72.4 1.3 fusion.75
  73.7 1.2 reshape.250
  74.9 1.2 fusion.76
  76.1 1.1 copy.42
  77.2 1.5 subtract_convert_fusion
  78.7 1.3 multiply_subtract_fusion
  80.2 2.3 fusion.3
  82.6 2.5 fusion.4
  85.1 2.6 fusion.49
  87.7 1.8 convolution_convert_fusion
  90.3 8.1 %scatter_custom_fusion = s32[3072]{0:T(1024)S(1)} fusion(s32[2048]{0:T(1024)S(1)} %bitcast.90, s32[2048]{0:T(1024)S(1)} %add_select_fusion, s32[]{:T(128)} %constant.66.clone.1), kind=kCustom, calls=%fused_computation.92 | custom fusion | bytes 12292 | tf_op jit(solution)/shard_map/scatter | solution.py:100
  98.4 41.4 %all-reduce.4.cloned.1.call-done = bf16[256,2048]{1,0:T(8,128)(2,1)} async-done(((bf16[256,2048]{1,0:T(8,128)(2,1)}), bf16[256,2048]{1,0:T(8,128)(2,1)}) %all-reduce.4.cloned.1.call-update) | async-done | bytes 1048592 | tf_op jit(solution)/shard_map/psum | solution.py:85
  139.8 1.7 fusion.24
  141.5 1.0 copy-done.1
  142.9 16.0 %gather_fusion = bf16[3072,2048]{1,0:T(8,128)(2,1)} fusion(bf16[257,2048]{1,0:T(8,128)(2,1)S(1)} %concatenate.20, s32[3072]{0:T(1024)S(1)} %fusion.62), kind=kCustom, calls=%fused_computation | custom fusion | bytes 25178112 | tf_op jit(solution)/shard_map/gather | solution.py:102
  158.9 5.6 %all-to-all-start = ((bf16[16,192,2048]{2,1,0:T(8,128)(2,1)}), bf16[16,192,2048]{2,1,0:T(8,128)(2,1)}, u32[]{:S(2)}, u32[]{:S(2)}) async-start(bf16[16,192,2048]{2,1,0:T(8,128)(2,1)} %bitcast.81), calls=%async_computation | async-start | bytes 25165824 | tf_op jit(solution)/shard_map/all_to_all | solution.py:103
  164.5 7.7 %reshape.288 = bf16[2,2048,512,1]{2,1,0,3:T(8,128)(2,1)} reshape(bf16[2,2048,2,256]{3,2,1,0:T(2,128)(2,1)} %param.22) | data formatting | bytes 8388608 | tf_op jit(solution)/shard_map/reshape | solution.py:109
  172.1 131.1 %all-to-all-done = bf16[16,192,2048]{2,1,0:T(8,128)(2,1)} async-done(((bf16[16,192,2048]{2,1,0:T(8,128)(2,1)}), bf16[16,192,2048]{2,1,0:T(8,128)(2,1)}, u32[]{:S(2)}, u32[]{:S(2)}) %all-to-all-start) | async-done | bytes 12582944 | tf_op jit(solution)/shard_map/all_to_all | solution.py:103
  303.3 12.5 %fusion.11 = f32[8,2,192,512]{3,2,0,1:T(8,128)} fusion(bf16[2,2048,512,1]{2,1,0,3:T(8,128)(2,1)} %reshape.288, bf16[8,2,192,2048]{3,2,1,0:T(8,128)(2,1)} %bitcast.19), kind=kOutput, calls=%fused_computation.21 | convolution fusion | flops 6442450944 | bytes 23068672 | tf_op jit(solution)/shard_map/wjcd,jdf->wjcf/dot_general | solution.py:106
  315.8 9.3 %convert_bitcast_fusion = bf16[8,2,192,2048]{3,2,0,1:T(8,128)(2,1)} fusion(bf16[2,256,2048]{2,1,0:T(8,128)(2,1)S(1)} %copy-done, f32[8,2,192,512]{3,2,0,1:T(8,128)} %fusion.11), kind=kOutput, calls=%fused_computation.7 | convolution fusion | flops 3232235520 | bytes 20971520 | tf_op jit(solution)/shard_map/wjcf,jfd->wjcd/dot_general | solution.py:115
  325.0 10.7 %copy.36 = bf16[8,2,192,2048]{3,2,1,0:T(8,128)(2,1)} copy(bf16[8,2,192,2048]{3,2,0,1:T(8,128)(2,1)} %convert_bitcast_fusion) | data formatting | bytes 25165824 | tf_op jit(solution)/shard_map/convert_element_type | solution.py:117
  335.8 5.5 all-to-all-start.1
  341.5 138.8 %all-to-all-done.1 = bf16[16,192,2048]{2,1,0:T(8,128)(2,1)} async-done(((bf16[16,192,2048]{2,1,0:T(8,128)(2,1)}), bf16[16,192,2048]{2,1,0:T(8,128)(2,1)}, u32[]{:S(2)}, u32[]{:S(2)}) %all-to-all-start.1) | async-done | bytes 12582944 | tf_op jit(solution)/shard_map/all_to_all | solution.py:119
  480.3 22.5 %gather_fusion.1 = bf16[2048,2048]{1,0:T(8,128)(2,1)} fusion(bf16[3072,2048]{1,0:T(8,128)(2,1)} %bitcast.26, s32[2048]{0:T(1024)S(1)} %broadcast_clamp_fusion), kind=kCustom, calls=%fused_computation.1 | custom fusion | bytes 16785408 | tf_op jit(solution)/shard_map/gather | solution.py:126
  502.8 12.2 %fusion = bf16[256,2048]{1,0:T(8,128)(2,1)} fusion(bf16[2048,2048]{1,0:T(8,128)(2,1)} %gather_fusion.1, f32[256,8]{1,0:T(8,128)S(1)} %copy.37), kind=kLoop, calls=%fused_computation.4 | loop fusion | flops 12058624 | bytes 9445376 | tf_op jit(solution)/shard_map/reduce_sum | solution.py:127
  515.4 1.1 slice_bitcast_fusion
  516.5 0.8 maximum_bitcast_fusion
  517.3 22.6 %reduce-scatter.2.cloned.1.call-done = bf16[256,512]{1,0:T(8,128)(2,1)} async-done(((bf16[256,2048]{1,0:T(8,128)(2,1)}), bf16[256,512]{1,0:T(8,128)(2,1)}) %reduce-scatter.2.cloned.1.call-update) | async-done | bytes 262160 | tf_op jit(solution)/shard_map/reduce_scatter | solution.py:128
  539.9 1.8 fusion.54
  (66 shorter events, 3.6 us)
Async XLA Ops:
  7.2 308.6 %copy-start = (bf16[2,256,2048]{2,1,0:T(8,128)(2,1)S(1)}, bf16[2,256,2048]{2,1,0:T(8,128)(2,1)}, u32[]{:S(2)}) copy-start(bf16[2,256,2048]{2,1,0:T(8,128)(2,1)} %param.23) | copy-start | bytes 6291460
  7.2 39.6 %all-gather.3.cloned.1.call-start = ((), (), s32[]{:S(2)}) async-start(), calls=%async_computation.5 | async-start | bytes 1310720 | tf_op jit(solution)/shard_map/all_gather | solution.py:45
  7.9 131.8 %all-reduce.4.cloned.1.call-start = ((), (), s32[]{:S(2)}) async-start(), calls=%async_computation.3 | async-start | bytes 2097152 | tf_op jit(solution)/shard_map/psum | solution.py:85
  14.6 26.1 %copy-start.7 = (s32[1,256,8]{2,1,0:T(8,128)}, s32[1,256,8]{2,1,0:T(8,128)S(1)}, u32[]{:S(2)}) copy-start(s32[1,256,8]{2,1,0:T(8,128)S(1)} %copy.33) | copy-start | bytes 24580
  32.7 13.1 %copy-start.15 = (f32[2,512]{1,0:T(2,128)S(1)}, f32[2,512]{1,0:T(2,128)}, u32[]{:S(2)}) copy-start(f32[2,512]{1,0:T(2,128)} %param.15) | copy-start | bytes 12292
  32.7 13.6 %copy-start.13 = (bf16[2,2048]{1,0:T(2,128)(2,1)S(1)}, bf16[2,2048]{1,0:T(2,128)(2,1)}, u32[]{:S(2)}) copy-start(bf16[2,2048]{1,0:T(2,128)(2,1)} %param.13) | copy-start | bytes 24580
  45.3 8.0 %copy-start.9 = (s32[16,16,128]{2,1,0:T(8,128)}, s32[16,16,128]{2,1,0:T(8,128)S(1)}, u32[]{:S(2)}) copy-start(s32[16,16,128]{2,1,0:T(8,128)S(1)} %reduce-window.6) | copy-start | bytes 393220
  53.3 1.2 copy-start.2
  77.2 3.0 copy-start.5
  80.2 2.3 copy-start.11
  82.5 2.5 copy-start.4
  85.1 2.7 copy-start.6
  87.7 1.8 copy-start.8
  87.7 2.4 copy-start.10
  87.7 52.0 %copy-start.3 = (bf16[1,256,2048]{2,1,0:T(8,128)(2,1)S(1)}, bf16[1,256,2048]{2,1,0:T(8,128)(2,1)}, u32[]{:S(2)}) copy-start(bf16[1,256,2048]{2,1,0:T(8,128)(2,1)} %all-gather.3.cloned.1.call-done) | copy-start | bytes 3145732
  141.5 1.0 copy-start.1
  158.9 144.4 %all-to-all-start = ((bf16[16,192,2048]{2,1,0:T(8,128)(2,1)}), bf16[16,192,2048]{2,1,0:T(8,128)(2,1)}, u32[]{:S(2)}, u32[]{:S(2)}) async-start(bf16[16,192,2048]{2,1,0:T(8,128)(2,1)} %bitcast.81), calls=%async_computation | async-start | bytes 25165824 | tf_op jit(solution)/shard_map/all_to_all | solution.py:103
  335.8 5.5 %copy-start.14 = (f32[1,256,8]{1,2,0:T(8,128)S(1)}, f32[1,256,8]{1,2,0:T(8,128)}, u32[]{:S(2)}) copy-start(f32[1,256,8]{1,2,0:T(8,128)} %param.21) | copy-start | bytes 24580
  335.8 144.5 %all-to-all-start.1 = ((bf16[16,192,2048]{2,1,0:T(8,128)(2,1)}), bf16[16,192,2048]{2,1,0:T(8,128)(2,1)}, u32[]{:S(2)}, u32[]{:S(2)}) async-start(bf16[16,192,2048]{2,1,0:T(8,128)(2,1)} %bitcast.80), calls=%async_computation.1 | async-start | bytes 25165824 | tf_op jit(solution)/shard_map/all_to_all | solution.py:119
  341.3 198.7 %reduce-scatter.2.cloned.1.call-start = ((), (), s32[]{:S(2)}) async-start(), calls=%async_computation.4 | async-start | bytes 1310720 | tf_op jit(solution)/shard_map/reduce_scatter | solution.py:128
  502.8 12.3 %copy-start.12 = (bf16[256,4,128]{2,0,1:T(8,128)(2,1)S(1)}, bf16[256,4,128]{2,0,1:T(8,128)(2,1)}, u32[]{:S(2)}) copy-start(bf16[256,4,128]{2,0,1:T(8,128)(2,1)} %copy-done.11) | copy-start | bytes 786436
Sparse Core Ops, SparseCore 0:
  9.6 30.6 all-gather.2
  89.7 50.0 all-reduce.3
  515.2 24.7 reduce-scatter.1
where the time goes:
time: 550 us; the launch traced here: 548 us
  waiting for transfers between devices  335 us (61%)
  local copies, waits for them, and re-layouts  105 us (19%)
  other arithmetic  33.7 us (6%)
  matrix products  33.4 us (6%)
  between operations  16.8 us (3%)
  blocking collectives  13.6 us (2%)
  starting transfers between devices  11.2 us (2%)
    all_to_all x1, waiting for transfers between devices, per_device(): lax.all_to_all(parts.reshape(experts, capacity, full_width), 'wide', spli...  139 us
    all_to_all x1, waiting for transfers between devices, per_device(): lax.all_to_all(outgoing, 'wide', split_axis=0, concat_axis=0, tiled=True)  131 us
    psum x1, waiting for transfers between devices, per_device(): lax.psum(partial_out.astype(jnp.bfloat16), 'narrow').astype(jnp.float32)  41.4 us
    reduce_scatter x1, waiting for transfers between devices, per_device(): lax.psum_scatter(combined.astype(jnp.bfloat16), 'narrow', scatter_dimensi...  22.6 us
    gather x1, local copies, waits for them, and re-layouts, per_device(): returned.reshape(experts * capacity, full_width)[target].astype(jnp.float32)  22.5 us
    gather x1, local copies, waits for them, and re-layouts, per_device(): outgoing = padded[source_row].reshape(experts, capacity, full_width)  16 us
    unnamed x35, local copies, waits for them, and re-layouts  15.7 us
    psum x1, blocking collectives, per_device(): lax.psum((jnp.sum(queries * queries, -1), jnp.sum(keys_new * keys_new, -1...  13.6 us
  transfers between devices with their start and end apart: 5, of which 4 were waited for; matrix products, arithmetic and copies ran while one was open for 10% of the time, Pallas kernels for 0%

commit v1 on v0

--- a/solution.py
+++ b/solution.py
@@ -4,6 +4,11 @@
 from jax.sharding import PartitionSpec as P
 
 HD = 128
+
+
+def summed_here(x, mesh_axis):
+    shards = lax.all_gather(x, mesh_axis)
+    return jnp.sum(shards, axis=0)
 
 
 def normalize(values, gain_row):
@@ -82,7 +87,7 @@
         .reshape(span_len, local_cols)
     )
     partial_out = jnp.dot(heads_out, w_out, preferred_element_type=jnp.float32)
-    attention = lax.psum(partial_out.astype(jnp.bfloat16), "narrow").astype(jnp.float32)
+    attention = summed_here(partial_out.astype(jnp.bfloat16), "narrow").astype(jnp.float32)
     after = (tokens.astype(jnp.float32) + attention).astype(jnp.bfloat16)
     after_own = lax.dynamic_slice_in_dim(after, column * share_cols, share_cols, 1)
     routed = normalize(after, norm_gain[1]).astype(jnp.bfloat16)

time: 550 us -> 576 us (1.047)
  other arithmetic: 33.7 us -> 46.7 us
  waiting for transfers between devices: 335 us -> 344 us
    all_gather x0 -> x1, waiting for transfers between devices: none -> 51.2 us  [summed_here(): shards = lax.all_gather(x, mesh_axis)]
    psum x1 -> x0, waiting for transfers between devices: 41.4 us -> none  [per_device(): lax.psum(partial_out.astype(jnp.bfloat16), 'narrow').astype(jnp.float32)]
    unnamed x35 -> x25, local copies, waits for them, and re-layouts: 15.7 us -> 15 us
  transfers between devices with their start and end apart: 5 -> 5, of which waited for: 4 -> 5; matrix products, arithmetic and copies ran while one was open for 10% -> 12% of each run, Pallas kernels for 0% -> 0%
where the time goes in v1:
time: 576 us; the launch traced here: 574 us
  waiting for transfers between devices  344 us (60%)
  local copies, waits for them, and re-layouts  109 us (19%)
  other arithmetic  46.7 us (8%)
  matrix products  33.4 us (6%)
  between operations  16.7 us (3%)
  blocking collectives  13.4 us (2%)
  starting transfers between devices  11.2 us (2%)
    all_to_all x1, waiting for transfers between devices, per_device(): lax.all_to_all(parts.reshape(experts, capacity, full_width), 'wide', spli...  139 us
    all_to_all x1, waiting for transfers between devices, per_device(): lax.all_to_all(outgoing, 'wide', split_axis=0, concat_axis=0, tiled=True)  131 us
    all_gather x1, waiting for transfers between devices, summed_here(): shards = lax.all_gather(x, mesh_axis)  51.2 us
    gather x1, local copies, waits for them, and re-layouts, per_device(): returned.reshape(experts * capacity, full_width)[target].astype(jnp.float32)  22.5 us
    reduce_scatter x1, waiting for transfers between devices, per_device(): lax.psum_scatter(combined.astype(jnp.bfloat16), 'narrow', scatter_dimensi...  21.8 us
    gather x1, local copies, waits for them, and re-layouts, per_device(): outgoing = padded[source_row].reshape(experts, capacity, full_width)  16 us
    unnamed x25, local copies, waits for them, and re-layouts  15 us
    psum x1, blocking collectives, per_device(): lax.psum((jnp.sum(queries * queries, -1), jnp.sum(keys_new * keys_new, -1...  13.4 us
  transfers between devices with their start and end apart: 5, of which 5 were waited for; matrix products, arithmetic and copies ran while one was open for 12% of the time, Pallas kernels for 0%

profile of v1, /device:TPU:0, one launch (start us, length us, event | category | flops | bytes accessed | tf_op | source)
XLA Modules:
  0.0 573.7 jit_solution(19708301416617871)
XLA Ops:
  8.0 1.2 dynamic_slice.9
  11.2 1.2 dynamic_slice.10
  13.7 8.9 %copy.24 = bf16[2048,3,512]{0,2,1:T(8,128)(2,1)} copy(bf16[2048,3,512]{2,0,1:T(8,128)(2,1)} %param.14) | data formatting | bytes 12582912 | tf_op args[2]
  22.6 4.5 fusion.74
  27.1 4.0 copy.45
  31.1 4.0 copy.31
  35.1 4.0 copy.23
  40.2 1.5 fusion.27
  41.8 5.0 fusion.39
  46.9 1.0 copy-done.2
  48.7 13.4 %all-reduce.1 = (f32[256]{0:T(256)S(1)}, f32[256]{0:T(256)S(1)}) all-reduce(f32[256]{0:T(256)S(1)} %get-tuple-element.7, f32[256]{0:T(256)S(1)} %get-tuple-element.6), channel_id=1, replica_groups=mesh['wide'=8,'narrow'=4] {'narrow'}, use_global_device_ids=true, to_apply=%region_4.0 | all-reduce | flops 512 | bytes 4096 | tf_op jit(solution)/shard_map/psum | solution.py:59
  62.1 2.3 multiply_multiply_fusion.1
  64.4 1.2 reshape.249
  65.7 1.3 fusion.75
  66.9 1.2 reshape.250
  68.1 1.2 fusion.76
  69.4 1.1 copy.42
  70.5 1.5 subtract_convert_fusion
  72.0 1.3 multiply_subtract_fusion
  73.5 2.3 fusion.3
  75.8 2.5 fusion.4
  78.3 2.6 fusion.49
  81.0 1.7 convolution_convert_fusion
  83.7 1.4 fusion.61
  85.0 8.1 %reduce-window.6 = s32[16,16,128]{2,1,0:T(8,128)S(1)} reduce-window(s32[16,16,128]{2,1,0:T(8,128)} %fusion.61, s32[]{:T(128)} %constant.56.clone.1), window={size=1x1x128 pad=0_0x0_0x127_0}, to_apply=%region_9.10 | reduce-window | flops 4161536 | bytes 262148 | tf_op jit(solution)/shard_map/reduce-window
  93.2 1.0 slice_reduce_fusion
  94.2 1.5 reduce-window.9
  95.6 1.3 broadcast_multiply_fusion
  96.9 1.5 copy.32
  98.4 1.6 mul.268
  102.2 8.4 %scatter_custom_fusion = s32[3072]{0:T(1024)S(1)} fusion(s32[2048]{0:T(1024)S(1)} %bitcast.92, s32[2048]{0:T(1024)} %add_select_fusion, s32[]{:T(128)} %constant.67.clone.1), kind=kCustom, calls=%fused_computation.92 | custom fusion | bytes 12800 | tf_op jit(solution)/shard_map/scatter | solution.py:105
  110.7 51.2 %all-gather.7.cloned.1.call-done = bf16[1024,2048]{1,0:T(8,128)(2,1)} async-done(((bf16[256,2048]{1,0:T(8,128)(2,1)}), bf16[1024,2048]{1,0:T(8,128)(2,1)}) %all-gather.7.cloned.1.call-update) | async-done | bytes 4194320 | tf_op jit(solution)/shard_map/all_gather | solution.py:10
  161.9 4.3 reduce_sum.81
  166.1 1.7 fusion.24
  169.2 16.0 %gather_fusion = bf16[3072,2048]{1,0:T(8,128)(2,1)} fusion(bf16[257,2048]{1,0:T(8,128)(2,1)S(1)} %concatenate.20, s32[3072]{0:T(1024)S(1)} %fusion.62), kind=kCustom, calls=%fused_computation | custom fusion | bytes 25178112 | tf_op jit(solution)/shard_map/gather | solution.py:107
  185.2 5.3 all-to-all-start
  190.6 7.7 %reshape.289 = bf16[2,2048,512,1]{2,1,0,3:T(8,128)(2,1)} reshape(bf16[2,2048,2,256]{3,2,1,0:T(2,128)(2,1)} %param.22) | data formatting | bytes 8388608 | tf_op jit(solution)/shard_map/reshape | solution.py:114
  198.2 131.3 %all-to-all-done = bf16[16,192,2048]{2,1,0:T(8,128)(2,1)} async-done(((bf16[16,192,2048]{2,1,0:T(8,128)(2,1)}), bf16[16,192,2048]{2,1,0:T(8,128)(2,1)}, u32[]{:S(2)}, u32[]{:S(2)}) %all-to-all-start) | async-done | bytes 12582944 | tf_op jit(solution)/shard_map/all_to_all | solution.py:108
  329.6 12.5 %fusion.11 = f32[8,2,192,512]{3,2,0,1:T(8,128)} fusion(bf16[2,2048,512,1]{2,1,0,3:T(8,128)(2,1)} %reshape.289, bf16[8,2,192,2048]{3,2,1,0:T(8,128)(2,1)} %bitcast.20), kind=kOutput, calls=%fused_computation.21 | convolution fusion | flops 6442450944 | bytes 23068672 | tf_op jit(solution)/shard_map/wjcd,jdf->wjcf/dot_general | solution.py:111
  342.1 9.3 %convert_bitcast_fusion = bf16[8,2,192,2048]{3,2,0,1:T(8,128)(2,1)} fusion(bf16[2,256,2048]{2,1,0:T(8,128)(2,1)S(1)} %copy-done, f32[8,2,192,512]{3,2,0,1:T(8,128)} %fusion.11), kind=kOutput, calls=%fused_computation.7 | convolution fusion | flops 3232235520 | bytes 20971520 | tf_op jit(solution)/shard_map/wjcf,jfd->wjcd/dot_general | solution.py:120
  351.4 10.7 %copy.36 = bf16[8,2,192,2048]{3,2,1,0:T(8,128)(2,1)} copy(bf16[8,2,192,2048]{3,2,0,1:T(8,128)(2,1)} %convert_bitcast_fusion) | data formatting | bytes 25165824 | tf_op jit(solution)/shard_map/convert_element_type | solution.py:122
  362.1 5.5 all-to-all-start.1
  368.0 138.5 %all-to-all-done.1 = bf16[16,192,2048]{2,1,0:T(8,128)(2,1)} async-done(((bf16[16,192,2048]{2,1,0:T(8,128)(2,1)}), bf16[16,192,2048]{2,1,0:T(8,128)(2,1)}, u32[]{:S(2)}, u32[]{:S(2)}) %all-to-all-start.1) | async-done | bytes 12582944 | tf_op jit(solution)/shard_map/all_to_all | solution.py:124
  506.6 22.5 %gather_fusion.1 = bf16[2048,2048]{1,0:T(8,128)(2,1)} fusion(bf16[3072,2048]{1,0:T(8,128)(2,1)} %bitcast.27, s32[2048]{0:T(1024)S(1)} %broadcast_clamp_fusion), kind=kCustom, calls=%fused_computation.1 | custom fusion | bytes 16785408 | tf_op jit(solution)/shard_map/gather | solution.py:131
  529.1 12.2 %fusion = bf16[256,2048]{1,0:T(8,128)(2,1)} fusion(bf16[2048,2048]{1,0:T(8,128)(2,1)} %gather_fusion.1, f32[256,8]{1,0:T(8,128)S(1)} %copy.37), kind=kLoop, calls=%fused_computation.4 | loop fusion | flops 12058624 | bytes 9445376 | tf_op jit(solution)/shard_map/reduce_sum | solution.py:132
  541.7 1.1 slice_bitcast_fusion
  543.6 21.8 %reduce-scatter.2.cloned.1.call-done = bf16[256,512]{1,0:T(8,128)(2,1)} async-done(((bf16[256,2048]{1,0:T(8,128)(2,1)}), bf16[256,512]{1,0:T(8,128)(2,1)}) %reduce-scatter.2.cloned.1.call-update) | async-done | bytes 262160 | tf_op jit(solution)/shard_map/reduce_scatter | solution.py:133
  565.4 1.8 fusion.54
  (57 shorter events, 9.7 us)
Async XLA Ops:
  7.2 334.9 %copy-start = (bf16[2,256,2048]{2,1,0:T(8,128)(2,1)S(1)}, bf16[2,256,2048]{2,1,0:T(8,128)(2,1)}, u32[]{:S(2)}) copy-start(bf16[2,256,2048]{2,1,0:T(8,128)(2,1)} %param.23) | copy-start | bytes 6291460
  7.2 33.1 %all-gather.5.cloned.1.call-start = ((), (), s32[]{:S(2)}) async-start(), calls=%async_computation.4 | async-start | bytes 1310720 | tf_op jit(solution)/shard_map/all_gather | solution.py:50
  7.9 153.9 %all-gather.7.cloned.1.call-start = ((), (), s32[]{:S(2)}) async-start(), calls=%async_computation.5 | async-start | bytes 5242880 | tf_op jit(solution)/shard_map/all_gather | solution.py:10
  31.1 8.0 %copy-start.10 = (f32[2,512]{1,0:T(2,128)S(1)}, f32[2,512]{1,0:T(2,128)}, u32[]{:S(2)}) copy-start(f32[2,512]{1,0:T(2,128)} %param.15) | copy-start | bytes 12292
  31.1 8.5 %copy-start.8 = (bf16[2,2048]{1,0:T(2,128)(2,1)S(1)}, bf16[2,2048]{1,0:T(2,128)(2,1)}, u32[]{:S(2)}) copy-start(bf16[2,2048]{1,0:T(2,128)(2,1)} %param.13) | copy-start | bytes 24580
  46.7 1.2 copy-start.2
  70.5 3.0 copy-start.5
  75.8 2.5 copy-start.4
  78.3 2.6 copy-start.6
  81.0 1.8 copy-start.7
  82.7 83.4 %copy-start.3 = (bf16[1,256,2048]{2,1,0:T(8,128)(2,1)S(1)}, bf16[1,256,2048]{2,1,0:T(8,128)(2,1)}, u32[]{:S(2)}) copy-start(bf16[1,256,2048]{2,1,0:T(8,128)(2,1)} %all-gather.5.cloned.1.call-done) | copy-start | bytes 3145732
  167.8 1.0 copy-start.1
  185.2 144.4 %all-to-all-start = ((bf16[16,192,2048]{2,1,0:T(8,128)(2,1)}), bf16[16,192,2048]{2,1,0:T(8,128)(2,1)}, u32[]{:S(2)}, u32[]{:S(2)}) async-start(bf16[16,192,2048]{2,1,0:T(8,128)(2,1)} %bitcast.82), calls=%async_computation | async-start | bytes 25165824 | tf_op jit(solution)/shard_map/all_to_all | solution.py:108
  362.1 5.8 %copy-start.9 = (f32[1,256,8]{1,2,0:T(8,128)S(1)}, f32[1,256,8]{1,2,0:T(8,128)}, u32[]{:S(2)}) copy-start(f32[1,256,8]{1,2,0:T(8,128)} %param.21) | copy-start | bytes 24580
  362.1 144.5 %all-to-all-start.1 = ((bf16[16,192,2048]{2,1,0:T(8,128)(2,1)}), bf16[16,192,2048]{2,1,0:T(8,128)(2,1)}, u32[]{:S(2)}, u32[]{:S(2)}) async-start(bf16[16,192,2048]{2,1,0:T(8,128)(2,1)} %bitcast.81), calls=%async_computation.1 | async-start | bytes 25165824 | tf_op jit(solution)/shard_map/all_to_all | solution.py:124
  367.5 197.8 %reduce-scatter.2.cloned.1.call-start = ((), (), s32[]{:S(2)}) async-start(), calls=%async_computation.3 | async-start | bytes 1310720 | tf_op jit(solution)/shard_map/reduce_scatter | solution.py:133
Sparse Core Ops, SparseCore 0:
  9.6 30.6 all-gather.4
  82.8 78.9 all-gather.6
  541.5 23.8 reduce-scatter.1
